TPU v7x, 256 devices: a whole 4x4x8 slice. The times are simulated.
256 devices in a mesh: seq: 32 (over z, y_hi, core), chan: 8 (over y_lo, x).
Axes of the slice: x: 4, y: 4 (y_hi: 2, y_lo: 2; y = y_hi * 2 + y_lo), z: 8, core: 2. Of those that a mesh axis runs over, the one named last changes fastest.
Arguments:
- tokens: bfloat16 [384, 512, 1024], P('chan', 'seq'), may hold values from -6 to 6
- gating: bfloat16 [384, 512, 1024], P(None, ('seq', 'chan')), may hold values from -6 to 6
- kernel: bfloat16 [384, 1024, 512], P('chan', 'seq'), may hold values from -6 to 6
- first_factor: bfloat16 [1024, 1024], replicated, may hold values from -0.1875 to 0.1875
- first_twiddle: float32 [512, 1024], P('seq'), may hold values from 0.5 to 1.5
- second_factor: bfloat16 [512, 512], replicated, may hold values from -0.25 to 0.25
- inverse_second: bfloat16 [512, 512], replicated, may hold values from -0.25 to 0.25
- inverse_twiddle: float32 [1024, 512], P('seq'), may hold values from 0.5 to 1.5
- inverse_first: bfloat16 [1024, 1024], replicated, may hold values from -0.1875 to 0.1875
- projection: bfloat16 [384, 384], replicated, may hold values from -0.3125 to 0.3125
Outputs:
- result: bfloat16 [384, 512, 1024], P(None, ('seq', 'chan'))
All inputs are finite; a program needn't handle non-finite values.
Results may differ from a plain program's by a relative error of at most 0.012.
Values may be sent and summed in bfloat16 or wider, within the bound.
A program may use at most 64 MiB of HBM per device.

v0:
```python
import jax
import jax.numpy as jnp
from jax import lax
from jax.sharding import PartitionSpec as P


def body(
    tokens,
    gating,
    kernel,
    first_factor,
    first_twiddle,
    second_factor,
    inverse_second,
    inverse_twiddle,
    inverse_first,
    projection,
):
    seq_count = lax.axis_size("seq")
    chan_count = lax.axis_size("chan")
    channels, local_rows, order_inner = tokens.shape
    order_outer = second_factor.shape[0]
    block_cols = order_inner // seq_count
    chan_rows = local_rows // chan_count
    first_split = first_factor.reshape(seq_count, block_cols, order_inner)
    forward = jnp.einsum("cab,skb->scka", tokens, first_split, preferred_element_type=jnp.float32)
    twiddle = first_twiddle.reshape(local_rows, seq_count, block_cols).transpose(1, 2, 0)
    forward = (forward * twiddle[:, None]).astype(jnp.bfloat16)
    forward = forward.reshape(seq_count, 1, channels, block_cols * local_rows)
    received = lax.all_to_all(forward, "seq", split_axis=0, concat_axis=1, tiled=True)
    received = received.reshape(seq_count, channels, block_cols, local_rows)
    second_split = second_factor.reshape(order_outer, seq_count, local_rows)
    spectrum = jnp.einsum(
        "scka,jsa->ckj", received, second_split, preferred_element_type=jnp.float32
    )
    scaled = (spectrum * kernel).astype(jnp.bfloat16)
    first_join = inverse_first.reshape(order_inner, seq_count, block_cols)
    inverse_split = inverse_second.reshape(seq_count, local_rows, order_outer)
    inverse = jnp.einsum("ckj,sij->scki", scaled, inverse_split, preferred_element_type=jnp.float32)
    twiddle_back = inverse_twiddle.reshape(block_cols, seq_count, local_rows).transpose(1, 0, 2)
    inverse = (inverse * twiddle_back[:, None]).astype(jnp.bfloat16)
    inverse = inverse.reshape(seq_count, 1, channels, block_cols * local_rows)
    returned = lax.all_to_all(inverse, "seq", split_axis=0, concat_axis=1, tiled=True)
    returned = returned.reshape(seq_count, channels, block_cols, local_rows)
    mixed_rows = jnp.einsum(
        "scki,bsk->cib", returned, first_join, preferred_element_type=jnp.float32
    ).astype(jnp.bfloat16)
    mixed_rows = mixed_rows.reshape(channels, chan_count, chan_rows, order_inner)
    mixed_rows = lax.all_to_all(mixed_rows, "chan", split_axis=1, concat_axis=0, tiled=True)
    mixed_rows = mixed_rows.reshape(channels * chan_count, chan_rows, order_inner)
    gated_rows = (mixed_rows.astype(jnp.float32) * gating.astype(jnp.float32)).astype(jnp.bfloat16)
    result_rows = jnp.einsum(
        "cab,ce->eab", gated_rows, projection, preferred_element_type=jnp.float32
    )
    return result_rows.astype(jnp.bfloat16)


def solution(mesh):
    return jax.shard_map(
        body,
        mesh=mesh,
        in_specs=(
            P("chan", "seq", None),
            P(None, ("seq", "chan"), None),
            P("chan", "seq", None),
            P(),
            P("seq", None),
            P(),
            P(),
            P("seq", None),
            P(),
            P(),
        ),
        out_specs=P(None, ("seq", "chan"), None),
        check_vma=False,
    )
```

profile of v0, /device:TPU:16, one launch (start us, length us, event | category | flops | bytes accessed | tf_op | source)
XLA Modules:
  0.0 208.6 jit_solution(16965171331436541552)
XLA Ops:
  0.0 0.0 copy-start
  0.0 1.1 reshape.50
  1.1 0.2 copy.74
  1.3 0.3 copy-done
  1.6 6.3 %fusion.1 = bf16[32,48,32,16]{1,2,3,0:T(8,128)(2,1)S(1)} fusion(f32[32,32,16]{1,2,0:T(8,128)S(1)} %bitcast.80, bf16[32,32,1024,1]{2,1,3,0:T(8,128)(2,1)S(1)} %bitcast.72, bf16[48,16,1024]{2,1,0:T(8,128)(2,1)} %param.10), kind=kOutput, calls=%fused_computation.3 | convolution fusion | flops 1612185600 | bytes 5308416 | tf_op jit(solution)/shard_map/cab,skb->scka/dot_general | solution.py:26
  8.0 3.9 %copy.35 = bf16[32,48,32,16]{1,3,2,0:T(8,128)(2,1)} copy(bf16[32,48,32,16]{1,2,3,0:T(8,128)(2,1)S(1)} %fusion.1) | data formatting | bytes 3145728 | tf_op jit(solution)/shard_map/convert_element_type | solution.py:28
  11.9 4.7 %copy.36 = bf16[32,1,48,512]{3,2,1,0:T(8,128)(2,1)} copy(bf16[32,1,48,512]{2,3,0,1:T(8,128)(2,1)} %bitcast.73) | data formatting | bytes 3145728 | tf_op jit(solution)/shard_map/reshape | solution.py:29
  16.5 0.0 copy-start.3
  16.5 0.0 copy-start.4
  16.5 11.7 %all-to-all-start = ((bf16[32,1,48,512]{3,2,1,0:T(8,128)(2,1)}), bf16[32,1,48,512]{3,2,1,0:T(8,128)(2,1)S(1)}, u32[]{:S(2)}, u32[]{:S(2)}) async-start(bf16[32,1,48,512]{3,2,1,0:T(8,128)(2,1)} %copy.36), calls=%async_computation | async-start | bytes 3145728 | tf_op jit(solution)/shard_map/all_to_all | solution.py:30
  28.3 0.0 copy-done.3
  28.3 0.2 copy.38
  28.5 0.0 copy-done.4
  28.5 0.1 copy.41
  28.6 0.2 copy.42
  28.8 38.6 %all-to-all-done = bf16[32,1,48,512]{3,2,1,0:T(8,128)(2,1)S(1)} async-done(((bf16[32,1,48,512]{3,2,1,0:T(8,128)(2,1)}), bf16[32,1,48,512]{3,2,1,0:T(8,128)(2,1)S(1)}, u32[]{:S(2)}, u32[]{:S(2)}) %all-to-all-start) | async-done | bytes 1572896 | tf_op jit(solution)/shard_map/all_to_all | solution.py:30
  67.4 3.2 %copy.37 = bf16[32,1,48,512]{2,3,0,1:T(8,128)(2,1)} copy(bf16[32,1,48,512]{3,2,1,0:T(8,128)(2,1)S(1)} %all-to-all-done) | data formatting | bytes 3145728 | tf_op jit(solution)/shard_map/all_to_all | solution.py:30
  70.6 0.0 copy-start.5
  70.6 0.0 copy-start.6
  70.6 12.8 %copy.39 = bf16[32,48,32,16]{2,3,0,1:T(8,128)(2,1)} copy(bf16[32,48,32,16]{1,3,2,0:T(8,128)(2,1)} %bitcast.74) | data formatting | bytes 3145728 | tf_op jit(solution)/shard_map/reshape | solution.py:31
  83.3 0.0 copy-done.5
  83.3 0.0 copy-done.6
  83.3 9.0 %fusion = bf16[32,48,32,16]{0,2,3,1:T(8,128)(2,1)} fusion(f32[32,32,16]{0,1,2:T(8,128)S(1)} %copy.42, bf16[48,32,512]{2,1,0:T(8,128)(2,1)S(1)} %copy-done.5, bf16[32,48,32,16]{2,3,0,1:T(8,128)(2,1)} %copy.39, bf16[512,32,16,1]{0,2,1,3:T(8,128)(2,1)S(1)} %bitcast.79, bf16[32,16,512]{2,1,0:T(8,128)(2,1)S(1)} %bitcast.81), kind=kOutput, calls=%fused_computation.1 | convolution fusion | flops 1614544896 | bytes 5832704 | tf_op jit(solution)/shard_map/ckj,sij->scki/dot_general | solution.py:39
  92.3 12.7 %copy.43 = bf16[32,48,32,16]{1,3,2,0:T(8,128)(2,1)} copy(bf16[32,48,32,16]{0,2,3,1:T(8,128)(2,1)} %fusion) | data formatting | bytes 3145728 | tf_op jit(solution)/shard_map/convert_element_type | solution.py:41
  105.1 4.7 %copy.44 = bf16[32,1,48,512]{3,2,1,0:T(8,128)(2,1)} copy(bf16[32,1,48,512]{2,3,0,1:T(8,128)(2,1)} %bitcast.75) | data formatting | bytes 3145728 | tf_op jit(solution)/shard_map/reshape | solution.py:42
  109.7 6.0 %all-to-all-start.1 = ((bf16[32,1,48,512]{3,2,1,0:T(8,128)(2,1)}), bf16[32,1,48,512]{3,2,1,0:T(8,128)(2,1)S(1)}, u32[]{:S(2)}, u32[]{:S(2)}) async-start(bf16[32,1,48,512]{3,2,1,0:T(8,128)(2,1)} %copy.44), calls=%async_computation.1 | async-start | bytes 3145728 | tf_op jit(solution)/shard_map/all_to_all | solution.py:43
  115.7 4.0 %copy.46 = bf16[1024,1024]{0,1:T(8,128)(2,1)} copy(bf16[1024,1024]{1,0:T(8,128)(2,1)} %param.18) | data formatting | bytes 4194304 | tf_op args[8]
  119.7 35.1 %all-to-all-done.1 = bf16[32,1,48,512]{3,2,1,0:T(8,128)(2,1)S(1)} async-done(((bf16[32,1,48,512]{3,2,1,0:T(8,128)(2,1)}), bf16[32,1,48,512]{3,2,1,0:T(8,128)(2,1)S(1)}, u32[]{:S(2)}, u32[]{:S(2)}) %all-to-all-start.1) | async-done | bytes 1572896 | tf_op jit(solution)/shard_map/all_to_all | solution.py:43
  154.9 4.7 %copy.45 = bf16[32,1,48,512]{0,3,2,1:T(8,128)(2,1)} copy(bf16[32,1,48,512]{3,2,1,0:T(8,128)(2,1)S(1)} %all-to-all-done.1) | data formatting | bytes 3145728 | tf_op jit(solution)/shard_map/all_to_all | solution.py:43
  159.5 8.5 %bitcast_convert_fusion = bf16[48,16,1024]{2,1,0:T(8,128)(2,1)} fusion(bf16[32,48,32,16]{0,3,2,1:T(8,128)(2,1)} %bitcast.76, bf16[1024,32,32]{0,2,1:T(8,128)(2,1)} %bitcast.77), kind=kOutput, calls=%fused_computation.6 | convolution fusion | flops 1611399168 | bytes 5242880 | tf_op jit(solution)/shard_map/scki,bsk->cib/dot_general | solution.py:45
  168.1 2.5 %reshape.59 = bf16[48,8,2,1024]{3,2,1,0:T(2,128)(2,1)S(1)} reshape(bf16[48,16,1024]{2,1,0:T(8,128)(2,1)} %bitcast_convert_fusion) | data formatting | bytes 3145728 | tf_op jit(solution)/shard_map/reshape | solution.py:48
  170.6 1.1 copy.48
  171.7 26.3 %all_to_all.12 = bf16[48,8,2,1024]{3,2,0,1:T(2,128)(2,1)S(1)} all-to-all(bf16[48,8,2,1024]{3,2,0,1:T(2,128)(2,1)S(1)} %copy.48), channel_id=1, replica_groups=mesh['seq'=32,'chan'=8] {'chan'}, dimensions={1} | all-to-all | bytes 3145728 | tf_op jit(solution)/shard_map/all_to_all | solution.py:49
  198.0 0.0 copy-start.2
  198.0 1.1 bitcast_convert_fusion.1
  199.1 0.3 copy-done.2
  199.4 0.0 copy-start.7
  199.4 1.9 fusion.2
  201.3 0.0 copy-done.7
  201.3 0.0 copy-start.1
  201.4 2.3 %fusion.13 = bf16[384,2,1024]{0,2,1:T(8,128)(2,1)} fusion(bf16[384,2,1024]{2,1,0:T(2,128)(2,1)S(1)} %fusion.2, bf16[384,384]{1,0:T(8,128)(2,1)S(1)} %copy-done.7), kind=kOutput, calls=%fused_computation.18 | convolution fusion | flops 604766208 | bytes 3440640 | tf_op jit(solution)/shard_map/cab,ce->eab/dot_general | solution.py:52
  203.7 4.9 %copy.50 = bf16[384,2,1024]{2,1,0:T(2,128)(2,1)} copy(bf16[384,2,1024]{0,2,1:T(8,128)(2,1)} %fusion.13) | data formatting | bytes 3145728 | tf_op jit(solution)/shard_map/convert_element_type | solution.py:55
  208.6 0.0 copy-done.1
Async XLA Ops:
  0.0 1.6 copy-start
  16.5 11.7 %copy-start.3 = (bf16[512,512]{1,0:T(8,128)(2,1)S(1)}, bf16[512,512]{1,0:T(8,128)(2,1)}, u32[]{:S(2)}) copy-start(bf16[512,512]{1,0:T(8,128)(2,1)} %param.15) | copy-start | bytes 1572868
  16.5 12.0 %copy-start.4 = (f32[32,512]{1,0:T(8,128)S(1)}, f32[32,512]{1,0:T(8,128)}, u32[]{:S(2)}) copy-start(f32[32,512]{1,0:T(8,128)} %param.17) | copy-start | bytes 196612
  16.5 50.9 %all-to-all-start = ((bf16[32,1,48,512]{3,2,1,0:T(8,128)(2,1)}), bf16[32,1,48,512]{3,2,1,0:T(8,128)(2,1)S(1)}, u32[]{:S(2)}, u32[]{:S(2)}) async-start(bf16[32,1,48,512]{3,2,1,0:T(8,128)(2,1)} %copy.36), calls=%async_computation | async-start | bytes 3145728 | tf_op jit(solution)/shard_map/all_to_all | solution.py:30
  70.6 12.8 %copy-start.5 = (bf16[48,32,512]{2,1,0:T(8,128)(2,1)S(1)}, bf16[48,32,512]{2,1,0:T(8,128)(2,1)}, u32[]{:S(2)}) copy-start(bf16[48,32,512]{2,1,0:T(8,128)(2,1)} %param.12) | copy-start | bytes 4718596
  70.6 12.8 %copy-start.6 = (bf16[512,512]{1,0:T(8,128)(2,1)S(1)}, bf16[512,512]{1,0:T(8,128)(2,1)}, u32[]{:S(2)}) copy-start(bf16[512,512]{1,0:T(8,128)(2,1)} %param.16) | copy-start | bytes 1572868
  109.7 45.1 %all-to-all-start.1 = ((bf16[32,1,48,512]{3,2,1,0:T(8,128)(2,1)}), bf16[32,1,48,512]{3,2,1,0:T(8,128)(2,1)S(1)}, u32[]{:S(2)}, u32[]{:S(2)}) async-start(bf16[32,1,48,512]{3,2,1,0:T(8,128)(2,1)} %copy.44), calls=%async_computation.1 | async-start | bytes 3145728 | tf_op jit(solution)/shard_map/all_to_all | solution.py:43
  198.0 1.4 copy-start.2
  199.4 1.9 copy-start.7
  201.3 7.3 %copy-start.1 = (bf16[1024,1024]{1,0:T(8,128)(2,1)S(1)}, bf16[1024,1024]{1,0:T(8,128)(2,1)}, u32[]{:S(2)}) copy-start(bf16[1024,1024]{1,0:T(8,128)(2,1)} %param.13) | copy-start | bytes 6291460
where the time goes:
time: 210 us; the launch traced here: 209 us
  waiting for transfers between devices  73.8 us (35%)
  local copies, waits for them, and re-layouts  61.5 us (29%)
  blocking collectives  26.3 us (13%)
  matrix products  26.2 us (12%)
  starting transfers between devices  17.7 us (8%)
  other arithmetic  3 us (1%)
    all_to_all x1, waiting for transfers between devices, body(): lax.all_to_all(forward, 'seq', split_axis=0, concat_axis=1, tiled=True)  38.6 us
    all_to_all x1, waiting for transfers between devices, body(): lax.all_to_all(inverse, 'seq', split_axis=0, concat_axis=1, tiled=True)  35.1 us
    all_to_all x1, blocking collectives, body(): lax.all_to_all(mixed_rows, 'chan', split_axis=1, concat_axis=0, tiled=True)  26.3 us
    reshape x1, local copies, waits for them, and re-layouts, body(): received = received.reshape(seq_count, channels, block_cols, local_rows)  12.8 us
    convert_element_type x1, local copies, waits for them, and re-layouts, body(): inverse = (inverse * twiddle_back[:, None]).astype(jnp.bfloat16)  12.7 us
    all_to_all x1, starting transfers between devices, body(): lax.all_to_all(forward, 'seq', split_axis=0, concat_axis=1, tiled=True)  11.7 us
    dot_general x1, matrix products, body(): jnp.einsum('ckj,sij->scki', scaled, inverse_split, preferred_element_type...  8.99 us
    dot_general x1, matrix products, body(): jnp.einsum('scki,bsk->cib', returned, first_join, preferred_element_type=...  8.55 us
  transfers between devices with their start and end apart: 2, of which 2 were waited for; matrix products, arithmetic and copies ran while one was open for 2% of the time, Pallas kernels for 0%

commit v1 on v0

--- a/solution.py
+++ b/solution.py
@@ -40,7 +40,10 @@
     twiddle_back = inverse_twiddle.reshape(block_cols, seq_count, local_rows).transpose(1, 0, 2)
     inverse = (inverse * twiddle_back[:, None]).astype(jnp.bfloat16)
     inverse = inverse.reshape(seq_count, 1, channels, block_cols * local_rows)
-    returned = lax.all_to_all(inverse, "seq", split_axis=0, concat_axis=1, tiled=True)
+    returned = jnp.concatenate(
+        lax.all_to_all(jnp.stack(jnp.split(inverse, lax.axis_size("seq"), axis=0)), "seq", 0, 0),
+        axis=1,
+    )
     returned = returned.reshape(seq_count, channels, block_cols, local_rows)
     mixed_rows = jnp.einsum(
         "scki,bsk->cib", returned, first_join, preferred_element_type=jnp.float32

time: 210 us -> 261 us (1.24)
  local copies, waits for them, and re-layouts: 61.5 us -> 112 us
    split x0 -> x34, local copies, waits for them, and re-layouts: none -> 40.1 us  [body(): jnp.split(inverse, lax.axis_size('seq'), axis=0)]
    unnamed x19 -> x104, local copies, waits for them, and re-layouts: 5.01 us -> 24.4 us
    convert_element_type x1 -> x0, local copies, waits for them, and re-layouts: 12.7 us -> none  [body(): inverse = (inverse * twiddle_back[:, None]).astype(jnp.bfloat16)]
    another operation x0 -> x33, local copies, waits for them, and re-layouts: none -> 8.55 us  [body(): jnp.stack(jnp.split(inverse, lax.axis_size('seq'), axis=0))]
    reshape x1 -> x0, local copies, waits for them, and re-layouts: 4.66 us -> none  [body(): inverse = inverse.reshape(seq_count, 1, channels, block_cols * local_rows)]
where the time goes in v1:
time: 261 us; the launch traced here: 260 us
  local copies, waits for them, and re-layouts  112 us (43%)
  waiting for transfers between devices  73.9 us (28%)
  matrix products  26.3 us (10%)
  blocking collectives  26.3 us (10%)
  starting transfers between devices  17.7 us (7%)
  other arithmetic  3 us (1%)
    split x34, local copies, waits for them, and re-layouts, body(): jnp.split(inverse, lax.axis_size('seq'), axis=0)  40.1 us
    all_to_all x1, waiting for transfers between devices, body(): lax.all_to_all(forward, 'seq', split_axis=0, concat_axis=1, tiled=True)  38.7 us
    all_to_all x1, waiting for transfers between devices, body(): lax.all_to_all(jnp.stack(jnp.split(inverse, lax.axis_size('seq'), axis=0)...  35.2 us
    all_to_all x1, blocking collectives, body(): lax.all_to_all(mixed_rows, 'chan', split_axis=1, concat_axis=0, tiled=True)  26.3 us
    unnamed x104, local copies, waits for them, and re-layouts  24.4 us
    reshape x1, local copies, waits for them, and re-layouts, body(): received = received.reshape(seq_count, channels, block_cols, local_rows)  12.8 us
    all_to_all x1, starting transfers between devices, body(): lax.all_to_all(forward, 'seq', split_axis=0, concat_axis=1, tiled=True)  11.7 us
    dot_general x1, matrix products, body(): jnp.einsum('ckj,sij->scki', scaled, inverse_split, preferred_element_type...  9 us
  transfers between devices with their start and end apart: 2, of which 2 were waited for; matrix products, arithmetic and copies ran while one was open for 2% of the time, Pallas kernels for 0%

profile of v1, /device:TPU:16, one launch (start us, length us, event | category | flops | bytes accessed | tf_op | source)
XLA Modules:
  0.0 260.1 jit_solution(13782792696622776411)
XLA Ops:
  0.0 1.1 reshape.105
  1.6 6.3 %fusion.1 = bf16[32,48,32,16]{1,2,3,0:T(8,128)(2,1)S(1)} fusion(f32[32,32,16]{1,2,0:T(8,128)S(1)} %bitcast.142, bf16[32,32,1024,1]{2,1,3,0:T(8,128)(2,1)S(1)} %bitcast.103, bf16[48,16,1024]{2,1,0:T(8,128)(2,1)} %param.10), kind=kOutput, calls=%fused_computation.3 | convolution fusion | flops 1612185600 | bytes 5308416 | tf_op jit(solution)/shard_map/cab,skb->scka/dot_general | solution.py:26
  8.0 3.9 %copy.66 = bf16[32,48,32,16]{1,3,2,0:T(8,128)(2,1)} copy(bf16[32,48,32,16]{1,2,3,0:T(8,128)(2,1)S(1)} %fusion.1) | data formatting | bytes 3145728 | tf_op jit(solution)/shard_map/convert_element_type | solution.py:28
  11.9 4.7 %copy.67 = bf16[32,1,48,512]{3,2,1,0:T(8,128)(2,1)} copy(bf16[32,1,48,512]{2,3,0,1:T(8,128)(2,1)} %bitcast.104) | data formatting | bytes 3145728 | tf_op jit(solution)/shard_map/reshape | solution.py:29
  16.6 11.7 %all-to-all-start = ((bf16[32,1,48,512]{3,2,1,0:T(8,128)(2,1)}), bf16[32,1,48,512]{3,2,1,0:T(8,128)(2,1)S(1)}, u32[]{:S(2)}, u32[]{:S(2)}) async-start(bf16[32,1,48,512]{3,2,1,0:T(8,128)(2,1)} %copy.67), calls=%async_computation | async-start | bytes 3145728 | tf_op jit(solution)/shard_map/all_to_all | solution.py:30
  28.8 38.7 %all-to-all-done = bf16[32,1,48,512]{3,2,1,0:T(8,128)(2,1)S(1)} async-done(((bf16[32,1,48,512]{3,2,1,0:T(8,128)(2,1)}), bf16[32,1,48,512]{3,2,1,0:T(8,128)(2,1)S(1)}, u32[]{:S(2)}, u32[]{:S(2)}) %all-to-all-start) | async-done | bytes 1572896 | tf_op jit(solution)/shard_map/all_to_all | solution.py:30
  67.4 3.1 %copy.68 = bf16[32,1,48,512]{2,3,0,1:T(8,128)(2,1)} copy(bf16[32,1,48,512]{3,2,1,0:T(8,128)(2,1)S(1)} %all-to-all-done) | data formatting | bytes 3145728 | tf_op jit(solution)/shard_map/all_to_all | solution.py:30
  70.6 12.8 %copy.70 = bf16[32,48,32,16]{2,3,0,1:T(8,128)(2,1)} copy(bf16[32,48,32,16]{1,3,2,0:T(8,128)(2,1)} %bitcast.105) | data formatting | bytes 3145728 | tf_op jit(solution)/shard_map/reshape | solution.py:31
  83.3 9.0 %fusion = bf16[32,48,32,16]{2,0,3,1:T(8,128)(2,1)} fusion(f32[32,32,16]{1,0,2:T(8,128)S(1)} %copy.73, bf16[48,32,512]{2,1,0:T(8,128)(2,1)S(1)} %copy-done.32, bf16[32,48,32,16]{2,3,0,1:T(8,128)(2,1)} %copy.70, bf16[512,32,16,1]{0,2,1,3:T(8,128)(2,1)S(1)} %bitcast.109, bf16[32,16,512]{2,1,0:T(8,128)(2,1)S(1)} %bitcast.143), kind=kOutput, calls=%fused_computation.1 | convolution fusion | flops 1614544896 | bytes 5832704 | tf_op jit(solution)/shard_map/ckj,sij->scki/dot_general | solution.py:39
  92.3 12.6 %fusion.20 = (bf16[1,48,32,16]{2,0,3,1:T(2,128)(2,1)S(1)}, bf16[1,48,32,16]{2,0,3,1:T(2,128)(2,1)S(1)}, bf16[1,48,32,16]{2,0,3,1:T(2,128)(2,1)S(1)}, bf16[1,48,3...) fusion(bf16[32,48,32,16]{2,0,3,1:T(8,128)(2,1)} %fusion), kind=kLoop, calls=%fused_computation.56 | loop fusion | bytes 1277952 | tf_op jit(solution)/shard_map/split | solution.py:44
  104.9 8.4 %fusion.19 = (bf16[1,48,32,16]{2,0,3,1:T(2,128)(2,1)}, bf16[1,48,32,16]{2,0,3,1:T(2,128)(2,1)}, bf16[1,48,32,16]{2,0,3,1:T(2,128)(2,1)}, bf16[1,48,32,16]{2,0,3,...) fusion(bf16[32,48,32,16]{2,0,3,1:T(8,128)(2,1)S(1)} %copy-done.2), kind=kLoop, calls=%fused_computation.55 | loop fusion | bytes 1867776 | tf_op jit(solution)/shard_map/split | solution.py:44
  113.4 1.3 copy.74
  114.8 0.6 constant_dynamic-update-slice_fusion.31
  115.4 1.3 copy.75
  116.8 1.3 copy.76
  118.2 1.3 copy.77
  119.6 1.3 copy.78
  122.0 0.7 copy.112
  123.2 0.7 copy.113
  124.3 0.7 copy.114
  125.4 0.7 copy.115
  126.6 0.7 copy.116
  127.7 0.7 copy.117
  128.9 0.7 copy.118
  129.6 1.3 copy.87
  130.9 0.7 copy.119
  132.2 0.6 copy.89
  141.8 0.6 constant_dynamic-update-slice_fusion.30
  145.0 0.6 constant_dynamic-update-slice_fusion.25
  145.6 0.6 constant_dynamic-update-slice_fusion.24
  146.2 0.6 constant_dynamic-update-slice_fusion.23
  146.8 0.6 constant_dynamic-update-slice_fusion.22
  147.5 0.6 constant_dynamic-update-slice_fusion.21
  148.1 0.6 constant_dynamic-update-slice_fusion.20
  148.7 0.6 constant_dynamic-update-slice_fusion.19
  149.3 0.6 constant_dynamic-update-slice_fusion.18
  161.2 6.0 %all-to-all-start.1 = ((bf16[32,1,1,48,512]{4,3,2,1,0:T(8,128)(2,1)}), bf16[32,1,1,48,512]{4,3,2,1,0:T(8,128)(2,1)S(1)}, u32[]{:S(2)}, u32[]{:S(2)}) async-start(bf16[32,1,1,48,512]{4,3,2,1,0:T(8,128)(2,1)} %constant_dynamic-update-slice_fusion), calls=%async_computation.1 | async-start | bytes 3145728 | tf_op jit(solution)/shard_map/all_to_all | solution.py:44
  167.2 4.0 %copy.139 = bf16[1024,1024]{0,1:T(8,128)(2,1)} copy(bf16[1024,1024]{1,0:T(8,128)(2,1)} %param.18) | data formatting | bytes 4194304 | tf_op args[8]
  171.2 35.2 %all-to-all-done.1 = bf16[32,1,1,48,512]{4,3,2,1,0:T(8,128)(2,1)S(1)} async-done(((bf16[32,1,1,48,512]{4,3,2,1,0:T(8,128)(2,1)}), bf16[32,1,1,48,512]{4,3,2,1,0:T(8,128)(2,1)S(1)}, u32[]{:S(2)}, u32[]{:S(2)}) %all-to-all-start.1) | async-done | bytes 1572896 | tf_op jit(solution)/shard_map/all_to_all | solution.py:44
  206.3 4.7 %copy.138 = bf16[32,1,1,48,512]{0,4,3,2,1:T(8,128)(2,1)} copy(bf16[32,1,1,48,512]{4,3,2,1,0:T(8,128)(2,1)S(1)} %all-to-all-done.1) | data formatting | bytes 3145728 | tf_op jit(solution)/shard_map/all_to_all | solution.py:44
  211.0 8.5 %bitcast_convert_fusion = bf16[48,16,1024]{2,1,0:T(8,128)(2,1)} fusion(bf16[32,48,32,16]{0,3,2,1:T(8,128)(2,1)} %bitcast.106, bf16[1024,32,32]{0,2,1:T(8,128)(2,1)} %bitcast.107), kind=kOutput, calls=%fused_computation.6 | convolution fusion | flops 1611399168 | bytes 5242880 | tf_op jit(solution)/shard_map/scki,bsk->cib/dot_general | solution.py:48
  219.6 2.5 reshape.112
  222.1 1.1 copy.141
  223.2 26.3 %all_to_all.23 = bf16[48,8,2,1024]{3,2,0,1:T(2,128)(2,1)S(1)} all-to-all(bf16[48,8,2,1024]{3,2,0,1:T(2,128)(2,1)S(1)} %copy.141), channel_id=1, replica_groups=mesh['seq'=32,'chan'=8] {'chan'}, dimensions={1} | all-to-all | bytes 3145728 | tf_op jit(solution)/shard_map/all_to_all | solution.py:52
  249.5 1.1 bitcast_convert_fusion.1
  250.9 1.9 fusion.2
  252.8 2.4 fusion.13
  255.2 4.9 %copy.143 = bf16[384,2,1024]{2,1,0:T(2,128)(2,1)} copy(bf16[384,2,1024]{0,2,1:T(8,128)(2,1)} %fusion.13) | data formatting | bytes 3145728 | tf_op jit(solution)/shard_map/convert_element_type | solution.py:58
  (145 shorter events, 27.9 us)
Async XLA Ops:
  0.0 1.6 copy-start
  16.5 11.7 %copy-start.22 = (bf16[512,512]{1,0:T(8,128)(2,1)S(1)}, bf16[512,512]{1,0:T(8,128)(2,1)}, u32[]{:S(2)}) copy-start(bf16[512,512]{1,0:T(8,128)(2,1)} %param.15) | copy-start | bytes 1572868
  16.6 12.0 %copy-start.31 = (f32[32,512]{1,0:T(8,128)S(1)}, f32[32,512]{1,0:T(8,128)}, u32[]{:S(2)}) copy-start(f32[32,512]{1,0:T(8,128)} %param.17) | copy-start | bytes 196612
  16.6 50.9 %all-to-all-start = ((bf16[32,1,48,512]{3,2,1,0:T(8,128)(2,1)}), bf16[32,1,48,512]{3,2,1,0:T(8,128)(2,1)S(1)}, u32[]{:S(2)}, u32[]{:S(2)}) async-start(bf16[32,1,48,512]{3,2,1,0:T(8,128)(2,1)} %copy.67), calls=%async_computation | async-start | bytes 3145728 | tf_op jit(solution)/shard_map/all_to_all | solution.py:30
  70.6 12.8 %copy-start.32 = (bf16[48,32,512]{2,1,0:T(8,128)(2,1)S(1)}, bf16[48,32,512]{2,1,0:T(8,128)(2,1)}, u32[]{:S(2)}) copy-start(bf16[48,32,512]{2,1,0:T(8,128)(2,1)} %param.12) | copy-start | bytes 4718596
  70.6 12.8 %copy-start.33 = (bf16[512,512]{1,0:T(8,128)(2,1)S(1)}, bf16[512,512]{1,0:T(8,128)(2,1)}, u32[]{:S(2)}) copy-start(bf16[512,512]{1,0:T(8,128)(2,1)} %param.16) | copy-start | bytes 1572868
  92.3 12.6 %copy-start.2 = (bf16[32,48,32,16]{2,0,3,1:T(8,128)(2,1)S(1)}, bf16[32,48,32,16]{2,0,3,1:T(8,128)(2,1)}, u32[]{:S(2)}) copy-start(bf16[32,48,32,16]{2,0,3,1:T(8,128)(2,1)} %fusion) | copy-start | bytes 4718596
  125.4 6.2 %copy-start.21 = (bf16[1,48,32,16]{2,0,3,1:T(2,128)(2,1)S(1)}, bf16[1,48,32,16]{2,0,3,1:T(2,128)(2,1)}, u32[]{:S(2)}) copy-start(bf16[1,48,32,16]{2,0,3,1:T(2,128)(2,1)} %get-tuple-element.22) | copy-start | bytes 147460
  126.6 5.6 %copy-start.20 = (bf16[1,48,32,16]{2,0,3,1:T(2,128)(2,1)S(1)}, bf16[1,48,32,16]{2,0,3,1:T(2,128)(2,1)}, u32[]{:S(2)}) copy-start(bf16[1,48,32,16]{2,0,3,1:T(2,128)(2,1)} %get-tuple-element.21) | copy-start | bytes 147460
  127.7 5.2 %copy-start.19 = (bf16[1,48,32,16]{2,0,3,1:T(2,128)(2,1)S(1)}, bf16[1,48,32,16]{2,0,3,1:T(2,128)(2,1)}, u32[]{:S(2)}) copy-start(bf16[1,48,32,16]{2,0,3,1:T(2,128)(2,1)} %get-tuple-element.20) | copy-start | bytes 147460
  128.9 4.6 %copy-start.18 = (bf16[1,48,32,16]{2,0,3,1:T(2,128)(2,1)S(1)}, bf16[1,48,32,16]{2,0,3,1:T(2,128)(2,1)}, u32[]{:S(2)}) copy-start(bf16[1,48,32,16]{2,0,3,1:T(2,128)(2,1)} %get-tuple-element.19) | copy-start | bytes 147460
  130.9 3.1 %copy-start.17 = (bf16[1,48,32,16]{2,0,3,1:T(2,128)(2,1)S(1)}, bf16[1,48,32,16]{2,0,3,1:T(2,128)(2,1)}, u32[]{:S(2)}) copy-start(bf16[1,48,32,16]{2,0,3,1:T(2,128)(2,1)} %get-tuple-element.18) | copy-start | bytes 147460
  132.1 2.5 copy-start.16
  132.8 2.3 copy-start.15
  133.4 2.3 copy-start.14
  133.9 2.3 copy-start.13
  134.5 2.3 copy-start.12
  135.0 2.3 copy-start.11
  135.6 2.3 copy-start.10
  136.2 2.3 copy-start.9
  136.7 2.3 copy-start.8
  137.3 2.3 copy-start.7
  137.8 2.4 copy-start.6
  138.4 2.4 copy-start.5
  138.9 2.4 copy-start.4
  139.6 5.4 %copy-start.23 = (bf16[1,1,1,48,512]{4,3,2,1,0:T(8,128)(2,1)S(1)}, bf16[1,1,1,48,512]{4,3,2,1,0:T(8,128)(2,1)}, u32[]{:S(2)}) copy-start(bf16[1,1,1,48,512]{4,3,2,1,0:T(8,128)(2,1)} %copy.112) | copy-start | bytes 147460
  140.0 5.6 %copy-start.24 = (bf16[1,1,1,48,512]{4,3,2,1,0:T(8,128)(2,1)S(1)}, bf16[1,1,1,48,512]{4,3,2,1,0:T(8,128)(2,1)}, u32[]{:S(2)}) copy-start(bf16[1,1,1,48,512]{4,3,2,1,0:T(8,128)(2,1)} %copy.113) | copy-start | bytes 147460
  140.0 6.2 %copy-start.25 = (bf16[1,1,1,48,512]{4,3,2,1,0:T(8,128)(2,1)S(1)}, bf16[1,1,1,48,512]{4,3,2,1,0:T(8,128)(2,1)}, u32[]{:S(2)}) copy-start(bf16[1,1,1,48,512]{4,3,2,1,0:T(8,128)(2,1)} %copy.114) | copy-start | bytes 147460
  140.1 6.8 %copy-start.26 = (bf16[1,1,1,48,512]{4,3,2,1,0:T(8,128)(2,1)S(1)}, bf16[1,1,1,48,512]{4,3,2,1,0:T(8,128)(2,1)}, u32[]{:S(2)}) copy-start(bf16[1,1,1,48,512]{4,3,2,1,0:T(8,128)(2,1)} %copy.115) | copy-start | bytes 147460
  140.1 7.4 %copy-start.27 = (bf16[1,1,1,48,512]{4,3,2,1,0:T(8,128)(2,1)S(1)}, bf16[1,1,1,48,512]{4,3,2,1,0:T(8,128)(2,1)}, u32[]{:S(2)}) copy-start(bf16[1,1,1,48,512]{4,3,2,1,0:T(8,128)(2,1)} %copy.116) | copy-start | bytes 147460
  140.2 7.9 %copy-start.28 = (bf16[1,1,1,48,512]{4,3,2,1,0:T(8,128)(2,1)S(1)}, bf16[1,1,1,48,512]{4,3,2,1,0:T(8,128)(2,1)}, u32[]{:S(2)}) copy-start(bf16[1,1,1,48,512]{4,3,2,1,0:T(8,128)(2,1)} %copy.117) | copy-start | bytes 147460
  140.2 8.5 %copy-start.29 = (bf16[1,1,1,48,512]{4,3,2,1,0:T(8,128)(2,1)S(1)}, bf16[1,1,1,48,512]{4,3,2,1,0:T(8,128)(2,1)}, u32[]{:S(2)}) copy-start(bf16[1,1,1,48,512]{4,3,2,1,0:T(8,128)(2,1)} %copy.118) | copy-start | bytes 147460
  140.2 9.1 %copy-start.30 = (bf16[1,1,1,48,512]{4,3,2,1,0:T(8,128)(2,1)S(1)}, bf16[1,1,1,48,512]{4,3,2,1,0:T(8,128)(2,1)}, u32[]{:S(2)}) copy-start(bf16[1,1,1,48,512]{4,3,2,1,0:T(8,128)(2,1)} %copy.119) | copy-start | bytes 147460
  161.2 45.1 %all-to-all-start.1 = ((bf16[32,1,1,48,512]{4,3,2,1,0:T(8,128)(2,1)}), bf16[32,1,1,48,512]{4,3,2,1,0:T(8,128)(2,1)S(1)}, u32[]{:S(2)}, u32[]{:S(2)}) async-start(bf16[32,1,1,48,512]{4,3,2,1,0:T(8,128)(2,1)} %constant_dynamic-update-slice_fusion), calls=%async_computation.1 | async-start | bytes 3145728 | tf_op jit(solution)/shard_map/all_to_all | solution.py:44
  249.5 1.4 copy-start.3
  250.9 1.9 copy-start.34
  252.8 7.3 %copy-start.1 = (bf16[1024,1024]{1,0:T(8,128)(2,1)S(1)}, bf16[1024,1024]{1,0:T(8,128)(2,1)}, u32[]{:S(2)}) copy-start(bf16[1024,1024]{1,0:T(8,128)(2,1)} %param.13) | copy-start | bytes 6291460
